TPU v7x, 32 devices: a whole 2x2x4 slice. The times are simulated.
32 devices in a mesh: expert: 16 (over z, y, core), dp: 2 (over x).
Axes of the slice: x: 2, y: 2, z: 4, core: 2. Of those that a mesh axis runs over, the one named last changes fastest.
Arguments:
- tokens: bfloat16 [2, 512, 2048], P('dp', 'expert'), may hold values from -6 to 6
- cotangent: bfloat16 [2, 512, 2048], P('dp', 'expert'), may hold values from -6 to 6
- expert_ids: int32 [2, 512, 8], P('dp', 'expert'), may hold values from 0 to 15, all different within a row; in each aligned block of 32 rows (0 to 31, 32 to 63, ..., all dimensions but the last counted through in order) at most 24 rows name the same one
- gate_probs: bfloat16 [2, 512, 8], P('dp', 'expert'), may hold values from 0.029907227 to 0.59765625
- alpha: float32 [1], replicated, may hold values from 0.4 to 1.2
- gamma: float32 [2048], replicated, may hold values from 0.5 to 1.5
- beta: float32 [2048], replicated, may hold values from -1.5 to 1.5
- w_in: bfloat16 [16, 2, 768, 2048], P('expert', None, 'dp'), may hold values from -0.125 to 0.125
- w_down: bfloat16 [16, 768, 2048], P('expert', 'dp'), may hold values from -0.21875 to 0.21875
Outputs:
- grad_tokens: bfloat16 [2, 512, 2048], P('dp', 'expert')
- grad_probs: bfloat16 [2, 512, 8], P('dp', 'expert')
- grad_down: bfloat16 [16, 768, 2048], P('expert', 'dp')
- grad_gamma: float32 [2048], replicated
- grad_beta: float32 [2048], replicated
- grad_alpha: float32 [1], replicated
Inputs may be any that keep to these rules, and one draw needn't show every extreme that they name: `expert_ids`: each token names 8 different experts; among the 32 tokens of one block no expert is named by more than 24 tokens, and in some block some expert is named by exactly 24.
All inputs are finite; a program needn't handle non-finite values.
Results may differ from a plain program's by a relative error of at most 0.008.
Values may be sent and summed in bfloat16 or wider, within the bound.
No kernel may reach another device: no remote copies, remote signals or barrier semaphores. Data moves between devices by JAX's collectives and lax.ppermute only.
A program may use at most 64 MiB of HBM per device.

v0:
```python
import jax
import jax.numpy as jnp
from jax import lax
from jax.sharding import PartitionSpec as P

residual_scale = 0.7071


def contract_width(left, right):
    return lax.dot_general(
        left, right, (((1,), (1,)), ((), ())), preferred_element_type=jnp.float32
    )


def slot_layout(ids_local, expert_count, capacity):
    token_count, top_count = ids_local.shape
    labels = jnp.arange(expert_count, dtype=jnp.int32)
    onehot = (ids_local[:, :, None] == labels[None, None, :]).astype(jnp.int32)
    picks = jnp.sum(onehot, axis=1)
    before = jnp.cumsum(picks, axis=0) - picks
    slots = jnp.sum(onehot * before[:, None, :], axis=2)
    position = ids_local * capacity + slots
    pairs = jnp.arange(token_count * top_count, dtype=jnp.int32)
    table = jnp.full((expert_count * capacity,), token_count * top_count, jnp.int32)
    table = table.at[position.reshape(-1)].set(pairs)
    return (position, table)


def shards(tokens, cotangent, expert_ids, gate_probs, alpha, gamma, beta, w_in, w_down):
    expert_count = lax.axis_size("expert")
    token_count = tokens.shape[1]
    top_count = expert_ids.shape[2]
    width = tokens.shape[2]
    capacity = 3 * token_count * top_count // (2 * expert_count)
    rows_total = expert_count * capacity
    inputs = tokens[0].astype(jnp.float32)
    squashed = jnp.tanh(alpha[0] * inputs)
    normed = (gamma * squashed + beta).astype(jnp.bfloat16)
    position, table = slot_layout(expert_ids[0], expert_count, capacity)
    source_token = table // top_count
    zero_row = jnp.zeros((1, width), jnp.bfloat16)
    normed_pad = jnp.concatenate([normed, zero_row], axis=0)
    cot_pad = jnp.concatenate([cotangent[0], zero_row], axis=0)
    prob_pad = jnp.concatenate([gate_probs[0].reshape(-1), jnp.zeros((1,), jnp.bfloat16)], axis=0)
    send_rows = normed_pad[source_token].reshape(expert_count, capacity, width)
    send_cot = cot_pad[source_token].reshape(expert_count, capacity, width)
    send_prob = prob_pad[table].reshape(expert_count, capacity)
    recv_rows, recv_cot, recv_prob = (
        lax.all_to_all(send_rows, "expert", split_axis=0, concat_axis=0, tiled=True),
        lax.all_to_all(send_cot, "expert", split_axis=0, concat_axis=0, tiled=True),
        lax.all_to_all(send_prob, "expert", split_axis=0, concat_axis=0, tiled=True),
    )
    in_rows = recv_rows.reshape(rows_total, width)
    cot_rows = recv_cot.reshape(rows_total, width)
    prob_rows = recv_prob.reshape(rows_total).astype(jnp.float32)
    gate_up, lower_full = (
        lax.all_gather(w_in, "dp", axis=2, tiled=True),
        lax.all_gather(w_down, "dp", axis=1, tiled=True),
    )
    gate_pre = contract_width(in_rows, gate_up[0, 0])
    up_value = contract_width(in_rows, gate_up[0, 1])
    w_gate = gate_up[0, 0]
    w_upper = gate_up[0, 1]
    w_lower = lower_full[0]
    sigma = jax.nn.sigmoid(gate_pre)
    activation = (gate_pre * sigma * up_value).astype(jnp.bfloat16)
    back = contract_width(cot_rows, w_lower)
    weight_row = residual_scale * prob_rows
    scaled_cot = (weight_row[:, None] * cot_rows.astype(jnp.float32)).astype(jnp.bfloat16)
    row_grad = residual_scale * jnp.sum(activation.astype(jnp.float32) * back, axis=1)
    d_act = weight_row[:, None] * back
    d_gate = (d_act * up_value * sigma * (1.0 + gate_pre * (1.0 - sigma))).astype(jnp.bfloat16)
    d_up = (d_act * gate_pre * sigma).astype(jnp.bfloat16)
    d_rows = (
        jnp.dot(d_gate, w_gate, preferred_element_type=jnp.float32)
        + jnp.dot(d_up, w_upper, preferred_element_type=jnp.float32)
    ).astype(jnp.bfloat16)
    back_rows, back_probs = (
        lax.all_to_all(
            d_rows.reshape(expert_count, capacity, width),
            "expert",
            split_axis=0,
            concat_axis=0,
            tiled=True,
        ),
        lax.all_to_all(
            row_grad.astype(jnp.bfloat16).reshape(expert_count, capacity),
            "expert",
            split_axis=0,
            concat_axis=0,
            tiled=True,
        ),
    )
    partial_grad = lax.dot_general(
        activation, scaled_cot, (((0,), (0,)), ((), ())), preferred_element_type=jnp.float32
    )
    grad_down = lax.psum_scatter(
        partial_grad[None].astype(jnp.bfloat16), "dp", scatter_dimension=1, tiled=True
    )
    picked = back_rows.reshape(rows_total, width)[position]
    grad_normed = jnp.sum(picked.astype(jnp.float32), axis=1)
    grad_probs = back_probs.reshape(rows_total)[position]
    gamma_part = jnp.sum(grad_normed * squashed, axis=0)
    beta_part = jnp.sum(grad_normed, axis=0)
    pre_grad = grad_normed * gamma * (1.0 - squashed * squashed)
    alpha_part = jnp.sum(pre_grad * inputs).reshape(1)
    grad_gamma, grad_beta, grad_alpha = lax.psum(
        (gamma_part, beta_part, alpha_part), ("expert", "dp")
    )
    grad_tokens = (cotangent[0].astype(jnp.float32) + alpha[0] * pre_grad).astype(jnp.bfloat16)
    return (grad_tokens[None], grad_probs[None], grad_down, grad_gamma, grad_beta, grad_alpha)


def solution(mesh):
    placed = (
        P("dp", "expert", None),
        P("dp", "expert", None),
        P("dp", "expert", None),
        P("dp", "expert", None),
        P(),
        P(),
        P(),
        P("expert", None, "dp", None),
        P("expert", "dp", None),
    )
    return jax.shard_map(
        shards,
        mesh=mesh,
        in_specs=placed,
        out_specs=(
            P("dp", "expert", None),
            P("dp", "expert", None),
            P("expert", "dp", None),
            P(),
            P(),
            P(),
        ),
        check_vma=False,
    )
```

profile of v0, /device:TPU:0, one launch (start us, length us, event | category | flops | bytes accessed | tf_op | source)
XLA Modules:
  0.0 256.3 jit_solution(2240395038127851113)
XLA Ops:
  7.3 0.7 all-gather.5.cloned.1.call-update
  8.0 0.1 copy.30
  8.1 0.1 reshape_squeeze.3
  8.2 0.1 copy.32
  8.3 0.1 copy.31
  8.3 0.1 mul.162
  8.5 0.1 copy.34
  8.6 0.1 copy.35
  8.7 0.1 reduce_sum.71
  8.8 1.4 scatter_custom_fusion
  10.2 2.8 %gather_fusion = bf16[384]{0:T(512)(128)(2,1)S(1)} fusion(bf16[257]{0:T(512)(128)(2,1)S(1)} %pad_maximum_fusion, s32[1024]{0:T(1024)S(1)} %get-tuple-element.35), kind=kCustom, calls=%fused_computation | custom fusion | bytes 3072 | tf_op jit(solution)/shard_map/gather | solution.py:47
  13.1 0.7 all_to_all.25
  13.8 7.4 %all-to-all-start = ((bf16[16,1,24]{2,1,0:T(2,128)(2,1)}), bf16[16,1,24]{2,1,0:T(2,128)(2,1)S(1)}, u32[]{:S(2)}, u32[]{:S(2)}) async-start(bf16[16,1,24]{2,1,0:T(2,128)(2,1)} %all_to_all.25), calls=%async_computation | async-start | bytes 16384 | tf_op jit(solution)/shard_map/all_to_all | solution.py:51
  21.8 0.1 fusion.19
  21.9 3.1 %gather_fusion.2 = bf16[384,2048]{1,0:T(8,128)(2,1)} fusion(bf16[33,2048]{1,0:T(8,128)(2,1)S(1)} %concatenate.11, s32[1024]{0:T(1024)S(1)} %get-tuple-element.34), kind=kCustom, calls=%fused_computation.2 | custom fusion | bytes 3147264 | tf_op jit(solution)/shard_map/gather | solution.py:45
  25.0 2.4 all-to-all-done
  27.5 3.7 %all-to-all-start.2 = ((bf16[16,24,2048]{2,1,0:T(8,128)(2,1)}), bf16[16,24,2048]{2,1,0:T(8,128)(2,1)S(1)}, u32[]{:S(2)}, u32[]{:S(2)}) async-start(bf16[16,24,2048]{2,1,0:T(8,128)(2,1)} %bitcast.8), calls=%async_computation.2 | async-start | bytes 3145728 | tf_op jit(solution)/shard_map/all_to_all | solution.py:49
  31.3 0.7 all-gather.3.cloned.1.call-update
  32.0 0.1 copy-done.1
  32.1 3.1 %gather_fusion.1 = bf16[384,2048]{1,0:T(8,128)(2,1)} fusion(bf16[33,2048]{1,0:T(8,128)(2,1)S(1)} %concatenate.10, s32[1024]{0:T(1024)S(1)} %get-tuple-element.34), kind=kCustom, calls=%fused_computation.1 | custom fusion | bytes 3147264 | tf_op jit(solution)/shard_map/gather | solution.py:46
  35.3 27.8 %all-to-all-done.2 = bf16[16,24,2048]{2,1,0:T(8,128)(2,1)S(1)} async-done(((bf16[16,24,2048]{2,1,0:T(8,128)(2,1)}), bf16[16,24,2048]{2,1,0:T(8,128)(2,1)S(1)}, u32[]{:S(2)}, u32[]{:S(2)}) %all-to-all-start.2) | async-done | bytes 1572896 | tf_op jit(solution)/shard_map/all_to_all | solution.py:49
  63.1 9.1 %all-to-all-start.1 = ((bf16[16,24,2048]{2,1,0:T(8,128)(2,1)}), bf16[16,24,2048]{2,1,0:T(8,128)(2,1)S(1)}, u32[]{:S(2)}, u32[]{:S(2)}) async-start(bf16[16,24,2048]{2,1,0:T(8,128)(2,1)} %bitcast.4), calls=%async_computation.1 | async-start | bytes 3145728 | tf_op jit(solution)/shard_map/all_to_all | solution.py:50
  72.3 0.1 mul.166
  72.4 20.3 %all-gather.5.cloned.1.call-done = bf16[1,2,768,2048]{3,2,1,0:T(8,128)(2,1)} async-done(((bf16[1,2,384,2048]{3,2,1,0:T(8,128)(2,1)}), bf16[1,2,768,2048]{3,2,1,0:T(8,128)(2,1)}) %all-gather.5.cloned.1.call-update) | async-done | bytes 6291472 | tf_op jit(solution)/shard_map/all_gather | solution.py:57
  92.7 4.6 %fusion.5 = f32[384,768]{1,0:T(8,128)} fusion(bf16[384,2048]{1,0:T(8,128)(2,1)S(1)} %bitcast.79, bf16[1,2,768,2048]{3,2,1,0:T(8,128)(2,1)} %all-gather.5.cloned.1.call-done), kind=kOutput, calls=%fused_computation.16 | convolution fusion | flops 1207959552 | bytes 5898240 | tf_op jit(solution)/shard_map/dot_general | solution.py:10
  97.3 2.5 fusion.3
  99.8 4.4 %all-to-all-done.1 = bf16[16,24,2048]{2,1,0:T(8,128)(2,1)S(1)} async-done(((bf16[16,24,2048]{2,1,0:T(8,128)(2,1)}), bf16[16,24,2048]{2,1,0:T(8,128)(2,1)S(1)}, u32[]{:S(2)}, u32[]{:S(2)}) %all-to-all-start.1) | async-done | bytes 1572896 | tf_op jit(solution)/shard_map/all_to_all | solution.py:50
  104.2 35.0 %all-gather.3.cloned.1.call-done = bf16[1,768,2048]{2,1,0:T(8,128)(2,1)} async-done(((bf16[1,384,2048]{2,1,0:T(8,128)(2,1)}), bf16[1,768,2048]{2,1,0:T(8,128)(2,1)}) %all-gather.3.cloned.1.call-update) | async-done | bytes 3145744 | tf_op jit(solution)/shard_map/all_gather | solution.py:58
  139.2 5.0 %multiply_reduce_fusion = (f32[384]{0:T(512)S(1)}, bf16[384,768]{1,0:T(8,128)(2,1)S(1)}, f32[384,768]{1,0:T(8,128)}) fusion(f32[384,768]{1,0:T(8,128)} %fusion.3, f32[384,768]{1,0:T(8,128)} %fusion.5, bf16[384,2048]{1,0:T(8,128)(2,1)S(1)} %bitcast.81, bf16[1,768,2048]{2,1,0:T(8,128)(2,1)} %all-gather.3.cloned.1.call-done), kind=kOutput, calls=%fused_computation.21 | convolution fusion | flops 1210613376 | bytes 8848896 | tf_op jit(solution)/shard_map/dot_general | solution.py:10
  144.2 3.6 %fusion.2 = bf16[1,768,2048]{2,1,0:T(8,128)(2,1)} fusion(bf16[384,768]{1,0:T(8,128)(2,1)S(1)} %get-tuple-element.30, bf16[384,2048]{1,0:T(8,128)(2,1)S(1)} %bitcast.82, f32[384]{0:T(512)S(1)} %mul.166), kind=kOutput, calls=%fused_computation.13 | convolution fusion | flops 1211891712 | bytes 5309952 | tf_op jit(solution)/shard_map/dot_general | solution.py:94
  147.9 0.7 convert_element_type.97
  148.6 5.6 %all-to-all-start.4 = ((bf16[16,1,24]{2,1,0:T(2,128)(2,1)}), bf16[16,1,24]{2,1,0:T(2,128)(2,1)S(1)}, u32[]{:S(2)}, u32[]{:S(2)}) async-start(bf16[16,1,24]{2,1,0:T(2,128)(2,1)} %convert_element_type.97), calls=%async_computation.4 | async-start | bytes 16384 | tf_op jit(solution)/shard_map/all_to_all | solution.py:86
  154.3 4.4 %fusion.4 = f32[384,2048]{1,0:T(8,128)S(1)} fusion(bf16[1,2,768,2048]{3,2,1,0:T(8,128)(2,1)} %all-gather.5.cloned.1.call-done, f32[384,768]{1,0:T(8,128)S(1)} %copy-done.8, f32[384,768]{1,0:T(8,128)S(1)} %copy-done.9, f32[384,768]{1,0:T(8,128)} %get-tuple-element.33, f32[384]{0:T(512)S(1)} %mul.166), kind=kOutput, calls=%fused_computation.15 | convolution fusion | flops 1211203584 | bytes 9831936 | tf_op jit(solution)/shard_map/dot_general | solution.py:75
  158.7 4.7 %add_convert_fusion = bf16[384,2048]{1,0:T(8,128)(2,1)} fusion(f32[384,2048]{1,0:T(8,128)S(1)} %fusion.4, bf16[1,2,768,2048]{3,2,1,0:T(8,128)(2,1)} %all-gather.5.cloned.1.call-done, f32[384,768]{1,0:T(8,128)S(1)} %copy-done.8, f32[384,768]{1,0:T(8,128)S(1)} %copy-done.10, f32[384]{0:T(512)S(1)} %mul.166), kind=kOutput, calls=%fused_computation.12 | convolution fusion | flops 1211596800 | bytes 10225152 | tf_op jit(solution)/shard_map/dot_general | solution.py:76
  163.4 6.0 %all-to-all-start.3 = ((bf16[16,24,2048]{2,1,0:T(8,128)(2,1)}), bf16[16,24,2048]{2,1,0:T(8,128)(2,1)S(1)}, u32[]{:S(2)}, u32[]{:S(2)}) async-start(bf16[16,24,2048]{2,1,0:T(8,128)(2,1)} %bitcast.12), calls=%async_computation.3 | async-start | bytes 3145728 | tf_op jit(solution)/shard_map/all_to_all | solution.py:79
  169.4 0.1 copy.37
  169.5 0.1 reshape.211
  169.6 0.1 reshape.182
  169.7 1.9 gather_fusion.4
  171.7 0.1 broadcast_in_dim.11
  171.8 0.7 copy.39
  172.4 28.9 %all-to-all-done.3 = bf16[16,24,2048]{2,1,0:T(8,128)(2,1)S(1)} async-done(((bf16[16,24,2048]{2,1,0:T(8,128)(2,1)}), bf16[16,24,2048]{2,1,0:T(8,128)(2,1)S(1)}, u32[]{:S(2)}, u32[]{:S(2)}) %all-to-all-start.3) | async-done | bytes 1572896 | tf_op jit(solution)/shard_map/all_to_all | solution.py:79
  201.4 1.4 gather_fusion.3
  202.8 0.7 fusion.6
  203.4 0.7 fusion.23
  204.2 0.2 convert_reduce_fusion
  204.3 44.7 %all-reduce.2 = (f32[2048]{0:T(1024)}, f32[2048]{0:T(1024)}, f32[1]{0:T(128)}) all-reduce(f32[2048]{0:T(1024)S(1)} %get-tuple-element.25, f32[2048]{0:T(1024)S(1)} %convert_reduce_fusion, f32[1]{0:T(128)} %bitcast.19), channel_id=1, replica_groups=mesh['expert'=16,'dp'=2] {'expert','dp'}, use_global_device_ids=true, to_apply=%region_8.9 | all-reduce | flops 4097 | bytes 32776 | tf_op jit(solution)/shard_map/psum | solution.py:107
  249.0 0.8 fusion.30
  (44 shorter events, 0.4 us)
Async XLA Ops:
  7.2 0.8 copy-start.6
  7.2 1.0 copy-start.4
  7.2 14.6 %copy-start = (bf16[1,32,2048]{2,1,0:T(8,128)(2,1)S(1)}, bf16[1,32,2048]{2,1,0:T(8,128)(2,1)}, u32[]{:S(2)}) copy-start(bf16[1,32,2048]{2,1,0:T(8,128)(2,1)} %param.9) | copy-start | bytes 393220
  7.2 14.6 %copy-start.3 = (f32[2048]{0:T(1024)S(1)}, f32[2048]{0:T(1024)}, u32[]{:S(2)}) copy-start(f32[2048]{0:T(1024)} %param.14) | copy-start | bytes 24580
  7.2 14.6 %copy-start.5 = (f32[2048]{0:T(1024)S(1)}, f32[2048]{0:T(1024)}, u32[]{:S(2)}) copy-start(f32[2048]{0:T(1024)} %param.15) | copy-start | bytes 24580
  7.2 85.5 %all-gather.5.cloned.1.call-start = ((), (), s32[]{:S(2)}) async-start(), calls=%async_computation.7 | async-start | bytes 9437184 | tf_op jit(solution)/shard_map/all_gather | solution.py:57
  13.8 13.7 %all-to-all-start = ((bf16[16,1,24]{2,1,0:T(2,128)(2,1)}), bf16[16,1,24]{2,1,0:T(2,128)(2,1)S(1)}, u32[]{:S(2)}, u32[]{:S(2)}) async-start(bf16[16,1,24]{2,1,0:T(2,128)(2,1)} %all_to_all.25), calls=%async_computation | async-start | bytes 16384 | tf_op jit(solution)/shard_map/all_to_all | solution.py:51
  27.5 35.6 %all-to-all-start.2 = ((bf16[16,24,2048]{2,1,0:T(8,128)(2,1)}), bf16[16,24,2048]{2,1,0:T(8,128)(2,1)S(1)}, u32[]{:S(2)}, u32[]{:S(2)}) async-start(bf16[16,24,2048]{2,1,0:T(8,128)(2,1)} %bitcast.8), calls=%async_computation.2 | async-start | bytes 3145728 | tf_op jit(solution)/shard_map/all_to_all | solution.py:49
  31.2 0.9 copy-start.1
  31.2 108.0 %all-gather.3.cloned.1.call-start = ((), (), s32[]{:S(2)}) async-start(), calls=%async_computation.6 | async-start | bytes 4718592 | tf_op jit(solution)/shard_map/all_gather | solution.py:58
  63.1 41.1 %all-to-all-start.1 = ((bf16[16,24,2048]{2,1,0:T(8,128)(2,1)}), bf16[16,24,2048]{2,1,0:T(8,128)(2,1)S(1)}, u32[]{:S(2)}, u32[]{:S(2)}) async-start(bf16[16,24,2048]{2,1,0:T(8,128)(2,1)} %bitcast.4), calls=%async_computation.1 | async-start | bytes 3145728 | tf_op jit(solution)/shard_map/all_to_all | solution.py:50
  72.2 177.6 %reduce-scatter.2.cloned.1.call-start = ((), (), s32[]{:S(2)}) async-start(), calls=%async_computation.8 | async-start | bytes 4718592 | tf_op jit(solution)/shard_map/reduce_scatter | solution.py:97
  92.7 4.6 %copy-start.7 = (bf16[1,2,768,2048]{3,2,1,0:T(8,128)(2,1)S(1)}, bf16[1,2,768,2048]{3,2,1,0:T(8,128)(2,1)}, u32[]{:S(2)}) copy-start(bf16[1,2,768,2048]{3,2,1,0:T(8,128)(2,1)} %all-gather.5.cloned.1.call-done) | copy-start | bytes 18874372
  147.9 6.4 %copy-start.8 = (f32[384,768]{1,0:T(8,128)S(1)}, f32[384,768]{1,0:T(8,128)}, u32[]{:S(2)}) copy-start(f32[384,768]{1,0:T(8,128)} %fusion.5) | copy-start | bytes 3538948
  147.9 6.4 %copy-start.9 = (f32[384,768]{1,0:T(8,128)S(1)}, f32[384,768]{1,0:T(8,128)}, u32[]{:S(2)}) copy-start(f32[384,768]{1,0:T(8,128)} %fusion.3) | copy-start | bytes 3538948
  148.6 14.8 %all-to-all-start.4 = ((bf16[16,1,24]{2,1,0:T(2,128)(2,1)}), bf16[16,1,24]{2,1,0:T(2,128)(2,1)S(1)}, u32[]{:S(2)}, u32[]{:S(2)}) async-start(bf16[16,1,24]{2,1,0:T(2,128)(2,1)} %convert_element_type.97), calls=%async_computation.4 | async-start | bytes 16384 | tf_op jit(solution)/shard_map/all_to_all | solution.py:86
  154.2 4.4 %copy-start.10 = (f32[384,768]{1,0:T(8,128)S(1)}, f32[384,768]{1,0:T(8,128)}, u32[]{:S(2)}) copy-start(f32[384,768]{1,0:T(8,128)} %get-tuple-element.33) | copy-start | bytes 3538948
  163.4 38.0 %all-to-all-start.3 = ((bf16[16,24,2048]{2,1,0:T(8,128)(2,1)}), bf16[16,24,2048]{2,1,0:T(8,128)(2,1)S(1)}, u32[]{:S(2)}, u32[]{:S(2)}) async-start(bf16[16,24,2048]{2,1,0:T(8,128)(2,1)} %bitcast.12), calls=%async_computation.3 | async-start | bytes 3145728 | tf_op jit(solution)/shard_map/all_to_all | solution.py:79
  202.7 46.3 %copy-start.2 = (bf16[1,32,2048]{2,1,0:T(8,128)(2,1)S(1)}, bf16[1,32,2048]{2,1,0:T(8,128)(2,1)}, u32[]{:S(2)}) copy-start(bf16[1,32,2048]{2,1,0:T(8,128)(2,1)} %param.10) | copy-start | bytes 393220
Sparse Core Ops, SparseCore 0:
  9.6 83.0 all-gather.4
  94.2 44.9 all-gather.2
  148.0 43.3 reduce-scatter.1
where the time goes:
time: 257 us; the launch traced here: 256 us
  waiting for transfers between devices  120 us (47%)
  blocking collectives  44.7 us (17%)
  starting transfers between devices  31.9 us (12%)
  matrix products  24.8 us (10%)
  local copies, waits for them, and re-layouts  17.1 us (7%)
  between operations  14.7 us (6%)
  other arithmetic  2.6 us (1%)
    psum x1, blocking collectives, shards(): lax.psum((gamma_part, beta_part, alpha_part), ('expert', 'dp'))  44.7 us
    all_gather x1, waiting for transfers between devices, shards(): lax.all_gather(w_down, 'dp', axis=1, tiled=True)  35 us
    all_to_all x1, waiting for transfers between devices, shards(): lax.all_to_all(d_rows.reshape(expert_count, capacity, width), 'expert', s...  28.9 us
    all_to_all x1, waiting for transfers between devices, shards(): lax.all_to_all(send_rows, 'expert', split_axis=0, concat_axis=0, tiled=True)  27.8 us
    all_gather x1, waiting for transfers between devices, shards(): lax.all_gather(w_in, 'dp', axis=2, tiled=True)  20.3 us
    dot_general x3, matrix products, contract_width(): lax.dot_general(left, right, (((1,), (1,)), ((), ())), preferred_element_...  12.1 us
    all_to_all x1, starting transfers between devices, shards(): lax.all_to_all(send_cot, 'expert', split_axis=0, concat_axis=0, tiled=True)  9.08 us
    all_to_all x1, starting transfers between devices, shards(): lax.all_to_all(send_prob, 'expert', split_axis=0, concat_axis=0, tiled=True)  7.39 us
  transfers between devices with their start and end apart: 8, of which 6 were waited for; matrix products, arithmetic and copies ran while one was open for 14% of the time, Pallas kernels for 0%

commit v1 on v0

--- a/solution.py
+++ b/solution.py
@@ -105,7 +105,7 @@
     pre_grad = grad_normed * gamma * (1.0 - squashed * squashed)
     alpha_part = jnp.sum(pre_grad * inputs).reshape(1)
     grad_gamma, grad_beta, grad_alpha = lax.psum(
-        (gamma_part, beta_part, alpha_part), ("expert", "dp")
+        lax.psum((gamma_part, beta_part, alpha_part), "dp"), "expert"
     )
     grad_tokens = (cotangent[0].astype(jnp.float32) + alpha[0] * pre_grad).astype(jnp.bfloat16)
     return (grad_tokens[None], grad_probs[None], grad_down, grad_gamma, grad_beta, grad_alpha)

time: 257 us -> 284 us (1.11)
  blocking collectives: 44.7 us -> 72 us
    psum x1 -> x2, blocking collectives: 44.7 us -> 72 us  [the longest x1 63.1 us: shards(): lax.psum(lax.psum((gamma_part, beta_part, alpha_part), 'dp'), 'expert')]
  transfers between devices with their start and end apart: 8 -> 8, of which waited for: 6 -> 6; matrix products, arithmetic and copies ran while one was open for 14% -> 12% of each run, Pallas kernels for 0% -> 0%
where the time goes in v1:
time: 284 us
  waiting for transfers between devices  120 us (42%)
  blocking collectives  72 us (25%)
  starting transfers between devices  31.9 us (11%)
  matrix products  24.8 us (9%)
  local copies, waits for them, and re-layouts  17.1 us (6%)
  between operations  14.7 us (5%)
    psum x1, blocking collectives, shards(): lax.psum(lax.psum((gamma_part, beta_part, alpha_part), 'dp'), 'expert')  63.1 us
    all_gather x1, waiting for transfers between devices, shards(): lax.all_gather(w_down, 'dp', axis=1, tiled=True)  35 us
    all_to_all x1, waiting for transfers between devices, shards(): lax.all_to_all(d_rows.reshape(expert_count, capacity, width), 'expert', s...  28.9 us
    all_to_all x1, waiting for transfers between devices, shards(): lax.all_to_all(send_rows, 'expert', split_axis=0, concat_axis=0, tiled=True)  27.8 us
    all_gather x1, waiting for transfers between devices, shards(): lax.all_gather(w_in, 'dp', axis=2, tiled=True)  20.3 us
    dot_general x3, matrix products, contract_width(): lax.dot_general(left, right, (((1,), (1,)), ((), ())), preferred_element_...  12.1 us
    all_to_all x1, starting transfers between devices, shards(): lax.all_to_all(send_cot, 'expert', split_axis=0, concat_axis=0, tiled=True)  9.08 us
    psum x1, blocking collectives, shards(): lax.psum((gamma_part, beta_part, alpha_part), 'dp')  8.88 us
  transfers between devices with their start and end apart: 8, of which 6 were waited for; matrix products, arithmetic and copies ran while one was open for 12% of the time, Pallas kernels for 0%

profile of v1, /device:TPU:0, one launch (start us, length us, event | category | flops | bytes accessed | tf_op | source)
XLA Modules:
  0.0 283.7 jit_solution(17510254273383719763)
XLA Ops:
  7.3 0.7 all-gather.5.cloned.1.call-update
  8.0 0.1 copy.30
  8.1 0.1 reshape_squeeze.3
  8.2 0.1 copy.32
  8.3 0.1 copy.31
  8.3 0.1 mul.162
  8.5 0.1 copy.34
  8.6 0.1 copy.35
  8.7 0.1 reduce_sum.71
  8.8 1.4 scatter_custom_fusion
  10.2 2.8 gather_fusion
  13.1 0.7 all_to_all.25
  13.8 7.4 %all-to-all-start = ((bf16[16,1,24]{2,1,0:T(2,128)(2,1)}), bf16[16,1,24]{2,1,0:T(2,128)(2,1)S(1)}, u32[]{:S(2)}, u32[]{:S(2)}) async-start(bf16[16,1,24]{2,1,0:T(2,128)(2,1)} %all_to_all.25), calls=%async_computation | async-start | bytes 16384 | tf_op jit(solution)/shard_map/all_to_all | solution.py:51
  21.9 3.1 %gather_fusion.2 = bf16[384,2048]{1,0:T(8,128)(2,1)} fusion(bf16[33,2048]{1,0:T(8,128)(2,1)S(1)} %concatenate.11, s32[1024]{0:T(1024)S(1)} %get-tuple-element.37), kind=kCustom, calls=%fused_computation.2 | custom fusion | bytes 3147264 | tf_op jit(solution)/shard_map/gather | solution.py:45
  25.0 2.4 all-to-all-done
  27.5 3.7 %all-to-all-start.2 = ((bf16[16,24,2048]{2,1,0:T(8,128)(2,1)}), bf16[16,24,2048]{2,1,0:T(8,128)(2,1)S(1)}, u32[]{:S(2)}, u32[]{:S(2)}) async-start(bf16[16,24,2048]{2,1,0:T(8,128)(2,1)} %bitcast.8), calls=%async_computation.2 | async-start | bytes 3145728 | tf_op jit(solution)/shard_map/all_to_all | solution.py:49
  31.3 0.7 all-gather.3.cloned.1.call-update
  32.0 0.1 copy-done.1
  32.1 3.1 %gather_fusion.1 = bf16[384,2048]{1,0:T(8,128)(2,1)} fusion(bf16[33,2048]{1,0:T(8,128)(2,1)S(1)} %concatenate.10, s32[1024]{0:T(1024)S(1)} %get-tuple-element.37), kind=kCustom, calls=%fused_computation.1 | custom fusion | bytes 3147264 | tf_op jit(solution)/shard_map/gather | solution.py:46
  35.3 27.8 %all-to-all-done.2 = bf16[16,24,2048]{2,1,0:T(8,128)(2,1)S(1)} async-done(((bf16[16,24,2048]{2,1,0:T(8,128)(2,1)}), bf16[16,24,2048]{2,1,0:T(8,128)(2,1)S(1)}, u32[]{:S(2)}, u32[]{:S(2)}) %all-to-all-start.2) | async-done | bytes 1572896 | tf_op jit(solution)/shard_map/all_to_all | solution.py:49
  63.1 9.1 %all-to-all-start.1 = ((bf16[16,24,2048]{2,1,0:T(8,128)(2,1)}), bf16[16,24,2048]{2,1,0:T(8,128)(2,1)S(1)}, u32[]{:S(2)}, u32[]{:S(2)}) async-start(bf16[16,24,2048]{2,1,0:T(8,128)(2,1)} %bitcast.4), calls=%async_computation.1 | async-start | bytes 3145728 | tf_op jit(solution)/shard_map/all_to_all | solution.py:50
  72.3 0.1 mul.166
  72.4 20.3 %all-gather.5.cloned.1.call-done = bf16[1,2,768,2048]{3,2,1,0:T(8,128)(2,1)} async-done(((bf16[1,2,384,2048]{3,2,1,0:T(8,128)(2,1)}), bf16[1,2,768,2048]{3,2,1,0:T(8,128)(2,1)}) %all-gather.5.cloned.1.call-update) | async-done | bytes 6291472 | tf_op jit(solution)/shard_map/all_gather | solution.py:57
  92.7 4.5 %fusion.5 = f32[384,768]{1,0:T(8,128)} fusion(bf16[384,2048]{1,0:T(8,128)(2,1)S(1)} %bitcast.79, bf16[1,2,768,2048]{3,2,1,0:T(8,128)(2,1)} %all-gather.5.cloned.1.call-done), kind=kOutput, calls=%fused_computation.16 | convolution fusion | flops 1207959552 | bytes 5898240 | tf_op jit(solution)/shard_map/dot_general | solution.py:10
  97.2 2.6 fusion.3
  99.8 4.4 %all-to-all-done.1 = bf16[16,24,2048]{2,1,0:T(8,128)(2,1)S(1)} async-done(((bf16[16,24,2048]{2,1,0:T(8,128)(2,1)}), bf16[16,24,2048]{2,1,0:T(8,128)(2,1)S(1)}, u32[]{:S(2)}, u32[]{:S(2)}) %all-to-all-start.1) | async-done | bytes 1572896 | tf_op jit(solution)/shard_map/all_to_all | solution.py:50
  104.2 35.0 %all-gather.3.cloned.1.call-done = bf16[1,768,2048]{2,1,0:T(8,128)(2,1)} async-done(((bf16[1,384,2048]{2,1,0:T(8,128)(2,1)}), bf16[1,768,2048]{2,1,0:T(8,128)(2,1)}) %all-gather.3.cloned.1.call-update) | async-done | bytes 3145744 | tf_op jit(solution)/shard_map/all_gather | solution.py:58
  139.2 5.0 %multiply_reduce_fusion = (f32[384]{0:T(512)S(1)}, bf16[384,768]{1,0:T(8,128)(2,1)S(1)}, f32[384,768]{1,0:T(8,128)}) fusion(f32[384,768]{1,0:T(8,128)} %fusion.3, f32[384,768]{1,0:T(8,128)} %fusion.5, bf16[384,2048]{1,0:T(8,128)(2,1)S(1)} %bitcast.81, bf16[1,768,2048]{2,1,0:T(8,128)(2,1)} %all-gather.3.cloned.1.call-done), kind=kOutput, calls=%fused_computation.21 | convolution fusion | flops 1210613376 | bytes 8848896 | tf_op jit(solution)/shard_map/dot_general | solution.py:10
  144.2 3.6 %fusion.2 = bf16[1,768,2048]{2,1,0:T(8,128)(2,1)} fusion(bf16[384,768]{1,0:T(8,128)(2,1)S(1)} %get-tuple-element.33, bf16[384,2048]{1,0:T(8,128)(2,1)S(1)} %bitcast.82, f32[384]{0:T(512)S(1)} %mul.166), kind=kOutput, calls=%fused_computation.13 | convolution fusion | flops 1211891712 | bytes 5309952 | tf_op jit(solution)/shard_map/dot_general | solution.py:94
  147.9 0.7 convert_element_type.97
  148.6 5.6 %all-to-all-start.4 = ((bf16[16,1,24]{2,1,0:T(2,128)(2,1)}), bf16[16,1,24]{2,1,0:T(2,128)(2,1)S(1)}, u32[]{:S(2)}, u32[]{:S(2)}) async-start(bf16[16,1,24]{2,1,0:T(2,128)(2,1)} %convert_element_type.97), calls=%async_computation.4 | async-start | bytes 16384 | tf_op jit(solution)/shard_map/all_to_all | solution.py:86
  154.3 4.4 %fusion.4 = f32[384,2048]{1,0:T(8,128)S(1)} fusion(bf16[1,2,768,2048]{3,2,1,0:T(8,128)(2,1)} %all-gather.5.cloned.1.call-done, f32[384,768]{1,0:T(8,128)S(1)} %copy-done.8, f32[384,768]{1,0:T(8,128)S(1)} %copy-done.9, f32[384,768]{1,0:T(8,128)} %get-tuple-element.36, f32[384]{0:T(512)S(1)} %mul.166), kind=kOutput, calls=%fused_computation.15 | convolution fusion | flops 1211203584 | bytes 9831936 | tf_op jit(solution)/shard_map/dot_general | solution.py:75
  158.7 4.7 %add_convert_fusion = bf16[384,2048]{1,0:T(8,128)(2,1)} fusion(f32[384,2048]{1,0:T(8,128)S(1)} %fusion.4, bf16[1,2,768,2048]{3,2,1,0:T(8,128)(2,1)} %all-gather.5.cloned.1.call-done, f32[384,768]{1,0:T(8,128)S(1)} %copy-done.8, f32[384,768]{1,0:T(8,128)S(1)} %copy-done.10, f32[384]{0:T(512)S(1)} %mul.166), kind=kOutput, calls=%fused_computation.12 | convolution fusion | flops 1211596800 | bytes 10225152 | tf_op jit(solution)/shard_map/dot_general | solution.py:76
  163.4 6.0 %all-to-all-start.3 = ((bf16[16,24,2048]{2,1,0:T(8,128)(2,1)}), bf16[16,24,2048]{2,1,0:T(8,128)(2,1)S(1)}, u32[]{:S(2)}, u32[]{:S(2)}) async-start(bf16[16,24,2048]{2,1,0:T(8,128)(2,1)} %bitcast.12), calls=%async_computation.3 | async-start | bytes 3145728 | tf_op jit(solution)/shard_map/all_to_all | solution.py:79
  169.5 0.1 copy.37
  169.5 0.1 reshape.211
  169.7 0.1 reshape.182
  169.8 1.9 gather_fusion.4
  171.7 0.1 broadcast_in_dim.11
  171.8 0.7 copy.39
  172.5 28.9 %all-to-all-done.3 = bf16[16,24,2048]{2,1,0:T(8,128)(2,1)S(1)} async-done(((bf16[16,24,2048]{2,1,0:T(8,128)(2,1)}), bf16[16,24,2048]{2,1,0:T(8,128)(2,1)S(1)}, u32[]{:S(2)}, u32[]{:S(2)}) %all-to-all-start.3) | async-done | bytes 1572896 | tf_op jit(solution)/shard_map/all_to_all | solution.py:79
  201.4 1.4 gather_fusion.3
  202.8 0.7 fusion.6
  203.5 0.7 fusion.23
  204.2 0.2 convert_reduce_fusion
  204.4 8.9 %all-reduce.3 = (f32[2048]{0:T(1024)S(1)}, f32[2048]{0:T(1024)S(1)}, f32[1]{0:T(128)}) all-reduce(f32[2048]{0:T(1024)S(1)} %get-tuple-element.25, f32[2048]{0:T(1024)S(1)} %convert_reduce_fusion, f32[1]{0:T(128)} %bitcast.19), channel_id=1, replica_groups=mesh['expert'=16,'dp'=2] {'dp'}, use_global_device_ids=true, to_apply=%region_8.9 | all-reduce | flops 4097 | bytes 32776 | tf_op jit(solution)/shard_map/psum | solution.py:108
  213.3 63.1 %all-reduce.2 = (f32[2048]{0:T(1024)}, f32[2048]{0:T(1024)}, f32[1]{0:T(128)}) all-reduce(f32[2048]{0:T(1024)S(1)} %get-tuple-element.29, f32[2048]{0:T(1024)S(1)} %get-tuple-element.30, f32[1]{0:T(128)} %get-tuple-element.31), channel_id=1, replica_groups=mesh['expert'=16,'dp'=2] {'expert'}, use_global_device_ids=true, to_apply=%region_9.10 | all-reduce | flops 4097 | bytes 32776 | tf_op jit(solution)/shard_map/psum | solution.py:107
  276.4 0.8 fusion.30
  (45 shorter events, 0.5 us)
Async XLA Ops:
  7.2 0.8 copy-start.6
  7.2 1.0 copy-start.4
  7.2 14.6 %copy-start = (bf16[1,32,2048]{2,1,0:T(8,128)(2,1)S(1)}, bf16[1,32,2048]{2,1,0:T(8,128)(2,1)}, u32[]{:S(2)}) copy-start(bf16[1,32,2048]{2,1,0:T(8,128)(2,1)} %param.9) | copy-start | bytes 393220
  7.2 14.6 %copy-start.3 = (f32[2048]{0:T(1024)S(1)}, f32[2048]{0:T(1024)}, u32[]{:S(2)}) copy-start(f32[2048]{0:T(1024)} %param.14) | copy-start | bytes 24580
  7.2 14.6 %copy-start.5 = (f32[2048]{0:T(1024)S(1)}, f32[2048]{0:T(1024)}, u32[]{:S(2)}) copy-start(f32[2048]{0:T(1024)} %param.15) | copy-start | bytes 24580
  7.2 85.5 %all-gather.5.cloned.1.call-start = ((), (), s32[]{:S(2)}) async-start(), calls=%async_computation.7 | async-start | bytes 9437184 | tf_op jit(solution)/shard_map/all_gather | solution.py:57
  13.8 13.7 %all-to-all-start = ((bf16[16,1,24]{2,1,0:T(2,128)(2,1)}), bf16[16,1,24]{2,1,0:T(2,128)(2,1)S(1)}, u32[]{:S(2)}, u32[]{:S(2)}) async-start(bf16[16,1,24]{2,1,0:T(2,128)(2,1)} %all_to_all.25), calls=%async_computation | async-start | bytes 16384 | tf_op jit(solution)/shard_map/all_to_all | solution.py:51
  27.5 35.6 %all-to-all-start.2 = ((bf16[16,24,2048]{2,1,0:T(8,128)(2,1)}), bf16[16,24,2048]{2,1,0:T(8,128)(2,1)S(1)}, u32[]{:S(2)}, u32[]{:S(2)}) async-start(bf16[16,24,2048]{2,1,0:T(8,128)(2,1)} %bitcast.8), calls=%async_computation.2 | async-start | bytes 3145728 | tf_op jit(solution)/shard_map/all_to_all | solution.py:49
  31.2 0.9 copy-start.1
  31.2 108.0 %all-gather.3.cloned.1.call-start = ((), (), s32[]{:S(2)}) async-start(), calls=%async_computation.6 | async-start | bytes 4718592 | tf_op jit(solution)/shard_map/all_gather | solution.py:58
  63.1 41.1 %all-to-all-start.1 = ((bf16[16,24,2048]{2,1,0:T(8,128)(2,1)}), bf16[16,24,2048]{2,1,0:T(8,128)(2,1)S(1)}, u32[]{:S(2)}, u32[]{:S(2)}) async-start(bf16[16,24,2048]{2,1,0:T(8,128)(2,1)} %bitcast.4), calls=%async_computation.1 | async-start | bytes 3145728 | tf_op jit(solution)/shard_map/all_to_all | solution.py:50
  72.2 205.0 %reduce-scatter.2.cloned.1.call-start = ((), (), s32[]{:S(2)}) async-start(), calls=%async_computation.8 | async-start | bytes 4718592 | tf_op jit(solution)/shard_map/reduce_scatter | solution.py:97
  92.7 4.5 %copy-start.7 = (bf16[1,2,768,2048]{3,2,1,0:T(8,128)(2,1)S(1)}, bf16[1,2,768,2048]{3,2,1,0:T(8,128)(2,1)}, u32[]{:S(2)}) copy-start(bf16[1,2,768,2048]{3,2,1,0:T(8,128)(2,1)} %all-gather.5.cloned.1.call-done) | copy-start | bytes 18874372
  147.9 6.4 %copy-start.8 = (f32[384,768]{1,0:T(8,128)S(1)}, f32[384,768]{1,0:T(8,128)}, u32[]{:S(2)}) copy-start(f32[384,768]{1,0:T(8,128)} %fusion.5) | copy-start | bytes 3538948
  147.9 6.4 %copy-start.9 = (f32[384,768]{1,0:T(8,128)S(1)}, f32[384,768]{1,0:T(8,128)}, u32[]{:S(2)}) copy-start(f32[384,768]{1,0:T(8,128)} %fusion.3) | copy-start | bytes 3538948
  148.6 14.8 %all-to-all-start.4 = ((bf16[16,1,24]{2,1,0:T(2,128)(2,1)}), bf16[16,1,24]{2,1,0:T(2,128)(2,1)S(1)}, u32[]{:S(2)}, u32[]{:S(2)}) async-start(bf16[16,1,24]{2,1,0:T(2,128)(2,1)} %convert_element_type.97), calls=%async_computation.4 | async-start | bytes 16384 | tf_op jit(solution)/shard_map/all_to_all | solution.py:86
  154.3 4.4 %copy-start.10 = (f32[384,768]{1,0:T(8,128)S(1)}, f32[384,768]{1,0:T(8,128)}, u32[]{:S(2)}) copy-start(f32[384,768]{1,0:T(8,128)} %get-tuple-element.36) | copy-start | bytes 3538948
  163.4 38.0 %all-to-all-start.3 = ((bf16[16,24,2048]{2,1,0:T(8,128)(2,1)}), bf16[16,24,2048]{2,1,0:T(8,128)(2,1)S(1)}, u32[]{:S(2)}, u32[]{:S(2)}) async-start(bf16[16,24,2048]{2,1,0:T(8,128)(2,1)} %bitcast.12), calls=%async_computation.3 | async-start | bytes 3145728 | tf_op jit(solution)/shard_map/all_to_all | solution.py:79
  202.8 73.6 %copy-start.2 = (bf16[1,32,2048]{2,1,0:T(8,128)(2,1)S(1)}, bf16[1,32,2048]{2,1,0:T(8,128)(2,1)}, u32[]{:S(2)}) copy-start(bf16[1,32,2048]{2,1,0:T(8,128)(2,1)} %param.10) | copy-start | bytes 393220
Sparse Core Ops, SparseCore 0:
  9.6 83.0 all-gather.4
  94.2 44.9 all-gather.2
  148.0 43.3 reduce-scatter.1
